TPU v7x, 512 devices: a whole 4x4x16 slice. The times are simulated.
512 devices in a mesh: rep: 4 (over y), blk: 32 (over z, core), tp: 4 (over x).
Axes of the slice: x: 4, y: 4, z: 16, core: 2. Of those that a mesh axis runs over, the one named last changes fastest.
Arguments:
- hidden: bfloat16 [16, 2048], P('rep', 'blk'), may hold values from -64 to 64
- ln_gain: float32 [2, 2048], P(None, 'blk'), may hold values from 0.1 to 1.9
- w_qkv: bfloat16 [2, 2048, 3, 2048], P(None, 'blk', None, 'tp'), may hold values from -0.125 to 0.125
- w_fc1: bfloat16 [2, 2048, 8192], P(None, 'blk', 'tp'), may hold values from -0.125 to 0.125
- w_out: bfloat16 [2, 2048, 2048], P(None, 'tp', 'blk'), may hold values from -0.125 to 0.125
- w_fc2: bfloat16 [2, 8192, 2048], P(None, 'tp', 'blk'), may hold values from -0.0625 to 0.0625
- caches: bfloat16 [2, 2, 1024, 32, 2048], P(None, None, ('rep', 'blk'), None, 'tp'), may hold values from -110 to 110
- page_owner: int32 [1024], P(('rep', 'blk')), may hold values from 0 to 15, as said below
- page_used: int32 [1024], P(('rep', 'blk')), may hold values from 0 to 1, as said below
- page_fill: int32 [1024], P(('rep', 'blk')), may hold values from 0 to 32, as said below
- page_tail: int32 [1024], P(('rep', 'blk')), may hold values from 0 to 1
- positions: int32 [16], P('rep'), may hold values from 0 to 4095
Outputs:
- hidden_out: bfloat16 [16, 2048], P('rep', 'blk')
- caches_out: bfloat16 [2, 2, 1024, 32, 2048], P(None, None, ('rep', 'blk'), None, 'tp')
Inputs may be any that keep to these rules, and one draw needn't show every extreme that they name: `page_owner`: requests are numbered replica by replica, 4 to a replica. Each request has exactly one page with page_tail 1, which is used and lies among the pages of its own replica; other pages of a request may lie on any replica. `page_used`: every page with page_tail 1 is used. `page_fill`: A used page with page_tail 0 is full; a page with page_tail 1 holds fewer than 32 tokens; an unused page holds 0.
All inputs are finite; a program needn't handle non-finite values.
Results may differ from a plain program's by a relative error of at most 0.012.
The roundings to bfloat16 on the way count: a program that leaves them out, or rounds other values in their place, can miss the bound.
Values may be sent and summed in bfloat16 or wider, within the bound.
No kernel may reach another device: no remote copies, remote signals or barrier semaphores. Data moves between devices by JAX's collectives and lax.ppermute only.
A program may use at most 64 MiB of HBM per device.

v0:
```python
import jax
import jax.numpy as jnp
from jax import lax
from jax.sharding import PartitionSpec as P

D = 2048
HD = 64
ROT = 32
LAYERS = 2
PAGE = 32
EPSILON = 1e-05
LOWEST = -1e30


def combined_all(value, axis, join):
    pieces = jax.tree.map(lambda part: lax.all_gather(part, axis), value)
    head = jax.tree.map(lambda part: part[0], pieces)
    tail = jax.tree.map(lambda part: part[1:], pieces)
    so_far, _ = lax.scan(lambda so_far, piece: (join(so_far, piece), None), head, tail)
    return so_far


def rotate_heads(tensor, positions):
    half_rot = ROT // 2
    steps_f = jnp.arange(half_rot, dtype=jnp.float32)
    inverse = 10000.0 ** (-2.0 * steps_f / ROT)
    angles = positions.astype(jnp.float32)[:, None] * inverse[None, :]
    cosine = jnp.cos(angles)[:, None, :]
    sine_val = jnp.sin(angles)[:, None, :]
    first_half = tensor[..., :half_rot]
    second_half = tensor[..., half_rot:ROT]
    return jnp.concatenate(
        [
            first_half * cosine - second_half * sine_val,
            second_half * cosine + first_half * sine_val,
            tensor[..., ROT:],
        ],
        axis=-1,
    )


def page_partials(query_rows, key_pages, value_pages, valid):
    scores = jnp.einsum(
        "shd,sphd->shp", query_rows, key_pages, preferred_element_type=jnp.float32
    ) * HD ** (-0.5)
    scores = jnp.where(valid[:, None, :], scores, LOWEST)
    highest = jnp.max(scores, axis=-1)
    weights = jnp.where(valid[:, None, :], jnp.exp(scores - highest[..., None]), 0.0)
    totals = jnp.sum(weights, axis=-1)
    rounded = weights.astype(jnp.bfloat16)
    outputs = jnp.einsum("shp,sphd->shd", rounded, value_pages, preferred_element_type=jnp.float32)
    return (highest, totals, outputs)


def merge_parts(left_part, right_part):
    left_high, left_total, left_out = left_part
    right_high, right_total, right_out = right_part
    joined = jnp.maximum(left_high, right_high)
    left_factor = jnp.exp(left_high - joined)
    right_factor = jnp.exp(right_high - joined)
    return (
        joined,
        left_total * left_factor + right_total * right_factor,
        left_out * left_factor[..., None] + right_out * right_factor[..., None],
    )


def per_device(
    hidden,
    ln_gain,
    w_qkv,
    w_fc1,
    w_out,
    w_fc2,
    caches,
    page_owner,
    page_used,
    page_fill,
    page_tail,
    positions,
):
    req_rows = hidden.shape[0]
    slot_count = page_owner.shape[0]
    width = w_out.shape[1]
    heads = width // HD
    rep_count = lax.axis_size("rep")
    rep_index = lax.axis_index("rep")
    all_reqs = req_rows * rep_count
    offsets = jnp.arange(PAGE, dtype=jnp.int32)
    is_tail = page_tail == 1
    is_used = page_used == 1
    write_at = (offsets[None, :] == page_fill[:, None]) & is_tail[:, None]
    valid = is_used[:, None] & (offsets[None, :] < (page_fill + page_tail)[:, None])
    home_rows = page_owner - rep_index * req_rows
    pick_home = (
        (home_rows[:, None] == jnp.arange(req_rows, dtype=jnp.int32)[None, :]) & is_tail[:, None]
    ).astype(jnp.bfloat16)
    pick_owner = page_owner[:, None] == jnp.arange(all_reqs, dtype=jnp.int32)[None, :]
    pick_query = pick_owner.astype(jnp.bfloat16)
    own_mask = pick_owner & is_used[:, None]
    own_map = own_mask.astype(jnp.float32)
    state = hidden
    cache_list = []
    for layer in range(LAYERS):
        resid = state.astype(jnp.float32)
        average = lax.psum(jnp.sum(resid, axis=-1), "blk") / D
        centered = resid - average[:, None]
        variance = lax.psum(jnp.sum(centered * centered, axis=-1), "blk") / D
        normed = (
            centered * lax.rsqrt(variance + EPSILON)[:, None] * ln_gain[layer][None, :]
        ).astype(jnp.bfloat16)
        qkv_part = jnp.dot(
            normed,
            w_qkv[layer].reshape(normed.shape[1], 3 * width),
            preferred_element_type=jnp.float32,
        )
        inner_part = jnp.dot(normed, w_fc1[layer], preferred_element_type=jnp.float32)
        qkv_full, inner = lax.psum((qkv_part, inner_part), "blk")
        mlp_act = jax.nn.gelu(inner, approximate=True).astype(jnp.bfloat16)
        qkv_full = qkv_full.reshape(req_rows, 3, heads, HD)
        mlp_part = jnp.dot(mlp_act, w_fc2[layer], preferred_element_type=jnp.float32)
        queries = (
            rotate_heads(qkv_full[:, 0], positions).astype(jnp.bfloat16).reshape(req_rows, width)
        )
        new_keys = (
            rotate_heads(qkv_full[:, 1], positions).astype(jnp.bfloat16).reshape(req_rows, width)
        )
        new_values = qkv_full[:, 2].astype(jnp.bfloat16).reshape(req_rows, width)
        gathered = lax.all_gather(queries, "rep", axis=0, tiled=True)
        fresh = jnp.dot(
            pick_home,
            jnp.concatenate([new_keys, new_values], axis=1),
            preferred_element_type=jnp.float32,
        ).astype(jnp.bfloat16)
        key_pages = jnp.where(write_at[:, :, None], fresh[:, None, :width], caches[layer, 0])
        value_pages = jnp.where(write_at[:, :, None], fresh[:, None, width:], caches[layer, 1])
        cache_list.append(jnp.stack([key_pages, value_pages]))
        query_rows = (
            jnp.dot(pick_query, gathered, preferred_element_type=jnp.float32)
            .astype(jnp.bfloat16)
            .reshape(slot_count, heads, HD)
        )
        highest, totals, outputs = page_partials(
            query_rows,
            key_pages.reshape(slot_count, PAGE, heads, HD),
            value_pages.reshape(slot_count, PAGE, heads, HD),
            valid,
        )
        masked_high = jnp.where(is_used[:, None], highest, LOWEST)
        local_high = jnp.max(
            jnp.where(own_mask[:, :, None], masked_high[:, None, :], LOWEST), axis=0
        )
        slot_high = jnp.sum(jnp.where(own_mask[:, :, None], local_high[None, :, :], 0.0), axis=1)
        scale_w = jnp.where(is_used[:, None], jnp.exp(highest - slot_high), 0.0)
        local_total = jnp.einsum(
            "sr,sh->rh", own_map, totals * scale_w, precision=lax.Precision.HIGHEST
        )
        local_out = jnp.einsum(
            "sr,shd->rhd", own_map, outputs * scale_w[..., None], precision=lax.Precision.HIGHEST
        )
        merged_high, merged_total, merged_out = combined_all(
            (local_high, local_total, local_out), ("rep", "blk"), merge_parts
        )
        req_total = lax.dynamic_slice_in_dim(merged_total, rep_index * req_rows, req_rows, 0)
        req_out = lax.dynamic_slice_in_dim(merged_out, rep_index * req_rows, req_rows, 0)
        attended = (req_out / req_total[..., None]).reshape(req_rows, width).astype(jnp.bfloat16)
        attn_part = jnp.dot(attended, w_out[layer], preferred_element_type=jnp.float32)
        branch_total = lax.psum(attn_part + mlp_part, "tp")
        state = (resid + branch_total).astype(jnp.bfloat16)
    return (state, jnp.stack(cache_list))


def solution(mesh):
    in_specs = (
        P("rep", "blk"),
        P(None, "blk"),
        P(None, "blk", None, "tp"),
        P(None, "blk", "tp"),
        P(None, "tp", "blk"),
        P(None, "tp", "blk"),
        P(None, None, ("rep", "blk"), None, "tp"),
        P(("rep", "blk")),
        P(("rep", "blk")),
        P(("rep", "blk")),
        P(("rep", "blk")),
        P("rep"),
    )
    out_specs = (P("rep", "blk"), P(None, None, ("rep", "blk"), None, "tp"))
    return jax.shard_map(
        per_device, mesh=mesh, in_specs=in_specs, out_specs=out_specs, check_vma=False
    )
```

profile of v0, /device:TPU:2, one launch (start us, length us, event | category | flops | bytes accessed | tf_op | source)
XLA Modules:
  0.0 1091.6 jit_solution(14421208025836142521)
XLA Ops:
  8.0 54.7 %psum.70 = f32[4]{0:T(128)S(1)} all-reduce(f32[4]{0:T(128)S(1)} %convert_reduce_fusion.1), channel_id=1, replica_groups=mesh['rep'=4,'blk'=32,'tp'=4] {'blk'}, use_global_device_ids=true, to_apply=%region_1.0 | all-reduce | flops 4 | bytes 32 | tf_op jit(solution)/shard_map/psum | solution.py:106
  62.8 0.9 fusion.97
  63.6 45.8 %psum.71 = f32[4]{0:T(128)S(1)} all-reduce(f32[4]{0:T(128)S(1)} %fusion.97), channel_id=1, replica_groups=mesh['rep'=4,'blk'=32,'tp'=4] {'blk'}, use_global_device_ids=true, to_apply=%region_3.0 | all-reduce | flops 4 | bytes 32 | tf_op jit(solution)/shard_map/psum | solution.py:108
  110.2 1.0 fusion.132
  111.5 1.2 fusion.20
  112.6 0.9 fusion.119
  113.6 90.1 %all-reduce.1 = (f32[4,3,8,64]{3,2,1,0:T(8,128)S(1)}, f32[4,2048]{1,0:T(4,128)S(1)}) all-reduce(f32[4,3,8,64]{3,2,1,0:T(8,128)S(1)} %reshape.328, f32[4,2048]{1,0:T(4,128)S(1)} %fusion.20), channel_id=1, replica_groups=mesh['rep'=4,'blk'=32,'tp'=4] {'blk'}, use_global_device_ids=true, to_apply=%region_4.0 | all-reduce | flops 14336 | bytes 114688 | tf_op jit(solution)/shard_map/psum | solution.py:118
  209.5 12.4 %all-gather.6 = bf16[4,4,512]{2,1,0:T(4,128)(2,1)S(1)} all-gather(bf16[1,4,512]{2,1,0:T(4,128)(2,1)S(1)} %reshape.356), channel_id=1, replica_groups=mesh['rep'=4,'blk'=32,'tp'=4] {'rep'}, dimensions={0}, use_global_device_ids=true | all-gather | bytes 20480 | tf_op jit(solution)/shard_map/all_gather | solution.py:129
  223.1 1.3 fusion.131
  226.6 0.9 fusion.47
  229.0 82.1 %all-gather.8 = f32[128,16,8]{1,2,0:T(8,128)S(1)} all-gather(f32[1,16,8]{1,2,0:T(8,128)S(1)} %convolution_bitcast_fusion.1), channel_id=3, replica_groups=mesh['rep'=4,'blk'=32,'tp'=4] {'rep','blk'}, dimensions={0}, use_global_device_ids=true | all-gather | bytes 66048 | tf_op jit(solution)/shard_map/all_gather | solution.py:16
  311.2 80.5 %all-gather.7 = f32[128,16,8]{1,2,0:T(8,128)S(1)} all-gather(f32[1,16,8]{1,2,0:T(8,128)S(1)} %bitcast.159), channel_id=2, replica_groups=mesh['rep'=4,'blk'=32,'tp'=4] {'rep','blk'}, dimensions={0}, use_global_device_ids=true | all-gather | bytes 66048 | tf_op jit(solution)/shard_map/all_gather | solution.py:16
  391.8 0.8 slice.231
  392.7 7.1 slice.234
  399.8 145.0 %while.28 = (s32[]{:T(128)}, f32[16,8]{0,1:T(8,128)S(1)}, f32[16,8]{0,1:T(8,128)S(1)}, f32[16,8,64]{2,1,0:T(8,128)S(1)}, f32[127,16,8]{1,2,0:T(8,128)S(1)}, /*in...) while((s32[]{:T(128)}, f32[16,8]{0,1:T(8,128)S(1)}, f32[16,8]{0,1:T(8,128)S(1)}, ...), condition=%wide.region_10.11_spmd, body=%wide.region_9.10_spmd.sunk | while | flops 25346 | bytes 171109 | solution.py:19
  400.0 0.9 constant_dynamic-slice_fusion.6
  403.5 0.8 constant_dynamic-slice_fusion.6
  412.6 0.8 constant_dynamic-slice_fusion.6
  416.0 0.8 constant_dynamic-slice_fusion.6
  425.2 0.8 constant_dynamic-slice_fusion.6
  434.3 0.8 constant_dynamic-slice_fusion.6
  437.7 0.8 constant_dynamic-slice_fusion.6
  446.8 0.8 constant_dynamic-slice_fusion.6
  456.0 0.8 constant_dynamic-slice_fusion.6
  459.4 0.8 constant_dynamic-slice_fusion.6
  468.5 0.8 constant_dynamic-slice_fusion.6
  477.6 0.8 constant_dynamic-slice_fusion.6
  481.1 0.8 constant_dynamic-slice_fusion.6
  490.2 0.8 constant_dynamic-slice_fusion.6
  499.3 0.8 constant_dynamic-slice_fusion.6
  502.7 0.8 constant_dynamic-slice_fusion.6
  511.9 0.8 constant_dynamic-slice_fusion.6
  521.0 0.8 constant_dynamic-slice_fusion.6
  524.4 0.8 constant_dynamic-slice_fusion.6
  533.6 0.8 constant_dynamic-slice_fusion.6
  542.7 0.8 constant_dynamic-slice_fusion.6
  545.3 1.1 convolution_add_fusion.1
  546.4 8.6 psum.74
  555.1 46.2 %psum.75 = f32[4]{0:T(128)S(1)} all-reduce(f32[4]{0:T(128)S(1)} %get-tuple-element.178), channel_id=1, replica_groups=mesh['rep'=4,'blk'=32,'tp'=4] {'blk'}, use_global_device_ids=true, to_apply=%region_14.15 | all-reduce | flops 4 | bytes 32 | tf_op jit(solution)/shard_map/psum | solution.py:106
  601.8 45.8 %psum.76 = f32[4]{0:T(128)S(1)} all-reduce(f32[4]{0:T(128)S(1)} %fusion.94), channel_id=1, replica_groups=mesh['rep'=4,'blk'=32,'tp'=4] {'blk'}, use_global_device_ids=true, to_apply=%region_16.17 | all-reduce | flops 4 | bytes 32 | tf_op jit(solution)/shard_map/psum | solution.py:108
  647.6 1.2 fusion.17
  648.7 1.1 fusion.122
  650.0 90.3 %all-reduce = (f32[4,3,8,64]{3,2,0,1:T(8,128)S(1)}, f32[4,2048]{1,0:T(4,128)S(1)}) all-reduce(f32[4,3,8,64]{3,2,0,1:T(8,128)S(1)} %copy.83, f32[4,2048]{1,0:T(4,128)S(1)} %fusion.17), channel_id=1, replica_groups=mesh['rep'=4,'blk'=32,'tp'=4] {'blk'}, use_global_device_ids=true, to_apply=%region_17.18 | all-reduce | flops 14336 | bytes 114688 | tf_op jit(solution)/shard_map/psum | solution.py:118
  741.2 11.9 %all-gather.9 = bf16[4,4,512]{2,1,0:T(4,128)(2,1)S(1)} all-gather(bf16[1,4,512]{2,1,0:T(4,128)(2,1)S(1)} %reshape.362), channel_id=1, replica_groups=mesh['rep'=4,'blk'=32,'tp'=4] {'rep'}, dimensions={0}, use_global_device_ids=true | all-gather | bytes 20480 | tf_op jit(solution)/shard_map/all_gather | solution.py:129
  755.3 0.9 fusion.46
  756.4 81.7 %all-gather.11 = f32[128,16,8]{1,2,0:T(8,128)S(1)} all-gather(f32[1,16,8]{1,2,0:T(8,128)S(1)} %convolution_bitcast_fusion), channel_id=6, replica_groups=mesh['rep'=4,'blk'=32,'tp'=4] {'rep','blk'}, dimensions={0}, use_global_device_ids=true | all-gather | bytes 66048 | tf_op jit(solution)/shard_map/all_gather | solution.py:16
  838.2 80.9 %all-gather.10 = f32[128,16,8]{1,2,0:T(8,128)S(1)} all-gather(f32[1,16,8]{1,2,0:T(8,128)S(1)} %bitcast.160), channel_id=5, replica_groups=mesh['rep'=4,'blk'=32,'tp'=4] {'rep','blk'}, dimensions={0}, use_global_device_ids=true | all-gather | bytes 66048 | tf_op jit(solution)/shard_map/all_gather | solution.py:16
  919.4 1.1 pad_maximum_fusion
  921.4 7.2 slice.251
  928.5 144.9 %while.29 = (s32[]{:T(128)}, f32[16,8]{0,1:T(8,128)S(1)}, f32[16,8]{0,1:T(8,128)S(1)}, f32[16,8,64]{2,1,0:T(8,128)S(1)}, f32[127,16,8]{1,2,0:T(8,128)S(1)}, /*in...) while((s32[]{:T(128)}, f32[16,8]{0,1:T(8,128)S(1)}, f32[16,8]{0,1:T(8,128)S(1)}, ...), condition=%wide.region_23.24_spmd, body=%wide.region_22.23_spmd.sunk | while | flops 25346 | bytes 171109 | solution.py:19
  928.7 0.8 constant_dynamic-slice_fusion.7
  932.1 0.8 constant_dynamic-slice_fusion.7
  935.5 0.8 constant_dynamic-slice_fusion.7
  944.6 0.8 constant_dynamic-slice_fusion.7
  953.8 0.8 constant_dynamic-slice_fusion.7
  957.2 0.8 constant_dynamic-slice_fusion.7
  966.3 0.8 constant_dynamic-slice_fusion.7
  975.5 0.8 constant_dynamic-slice_fusion.7
  978.9 0.8 constant_dynamic-slice_fusion.7
  988.0 0.8 constant_dynamic-slice_fusion.7
  997.1 0.8 constant_dynamic-slice_fusion.7
  1000.6 0.8 constant_dynamic-slice_fusion.7
  1009.7 0.8 constant_dynamic-slice_fusion.7
  1074.1 10.1 psum.79
  (1364 shorter events, 273.9 us)
Async XLA Ops:
  7.2 219.5 %copy-start.4 = (s32[8]{0:T(128)S(1)}, s32[8]{0:T(128)}, u32[]{:S(2)}) copy-start(s32[8]{0:T(128)} %param.23) | copy-start | bytes 100
  7.2 384.6 %all-gather.15.cloned.1.call-start = ((), (), s32[]{:S(2)}) async-start(), calls=%async_computation | async-start | bytes 8454144 | tf_op jit(solution)/shard_map/all_gather | solution.py:16
  227.6 692.9 %all-gather.17.cloned.1.call-start = ((), (), s32[]{:S(2)}) async-start(), calls=%async_computation.1 | async-start | bytes 8454144 | tf_op jit(solution)/shard_map/all_gather | solution.py:16
  392.6 152.5 %copy-start.1 = (bf16[2,512,64]{1,2,0:T(8,128)(2,1)S(1)}, bf16[2,512,64]{1,2,0:T(8,128)(2,1)}, u32[]{:S(2)}) copy-start(bf16[2,512,64]{1,2,0:T(8,128)(2,1)} %param.20) | copy-start | bytes 393220
  392.6 162.3 %copy-start.3 = (bf16[4,64]{1,0:T(4,128)(2,1)S(1)}, bf16[4,64]{1,0:T(4,128)(2,1)}, u32[]{:S(2)}) copy-start(bf16[4,64]{1,0:T(4,128)(2,1)} %param.16) | copy-start | bytes 1540
  399.8 519.3 %copy-start = (bf16[2,2,8,32,512]{4,3,2,1,0:T(8,128)(2,1)S(1)}, bf16[2,2,8,32,512]{4,3,2,1,0:T(8,128)(2,1)}, u32[]{:S(2)}) copy-start(bf16[2,2,8,32,512]{4,3,2,1,0:T(8,128)(2,1)} %param.22) | copy-start | bytes 3145732
  921.3 152.4 %copy-start.2 = (bf16[2,512,64]{1,2,0:T(8,128)(2,1)S(1)}, bf16[2,512,64]{1,2,0:T(8,128)(2,1)}, u32[]{:S(2)}) copy-start(bf16[2,512,64]{1,2,0:T(8,128)(2,1)} %param.20) | copy-start | bytes 393220
  921.3 152.5 %copy-start.5 = (bf16[2,2048,64]{1,2,0:T(8,128)(2,1)S(1)}, bf16[2,2048,64]{1,2,0:T(8,128)(2,1)}, u32[]{:S(2)}) copy-start(bf16[2,2048,64]{1,2,0:T(8,128)(2,1)} %param.21) | copy-start | bytes 1572868
Sparse Core Ops, SparseCore 0:
  227.7 143.5 all-gather.14
  756.4 142.3 all-gather.16
where the time goes:
time: 1100 us; the launch traced here: 1090 us
  blocking collectives  741 us (67%)
  local copies, waits for them, and re-layouts  275 us (25%)
  other arithmetic  43.7 us (4%)
  between operations  14.3 us (1%)
    all_gather x4, blocking collectives, combined_all(): pieces = jax.tree.map(lambda part: lax.all_gather(part, axis), value)  325 us
    dynamic_slice x254, local copies, waits for them, and re-layouts, combined_all(): lax.scan(lambda so_far, piece: (join(so_far, piece), None), head, tail)  215 us
    psum x2, blocking collectives, per_device(): qkv_full, inner = lax.psum((qkv_part, inner_part), 'blk')  180 us
    psum x2, blocking collectives, per_device(): average = lax.psum(jnp.sum(resid, axis=-1), 'blk') / D  101 us
    psum x2, blocking collectives, per_device(): variance = lax.psum(jnp.sum(centered * centered, axis=-1), 'blk') / D  91.6 us
    add x254, other arithmetic, merge_parts(): left_out * left_factor[..., None] + right_out * right_factor[..., None]  28.1 us
    all_gather x2, blocking collectives, per_device(): gathered = lax.all_gather(queries, 'rep', axis=0, tiled=True)  24.4 us
  transfers between devices with their start and end apart: 2, of which 0 were waited for; matrix products, arithmetic and copies ran while one was open for 0% of the time, Pallas kernels for 0%

commit v1 on v0

--- a/solution.py
+++ b/solution.py
@@ -126,7 +126,32 @@
             rotate_heads(qkv_full[:, 1], positions).astype(jnp.bfloat16).reshape(req_rows, width)
         )
         new_values = qkv_full[:, 2].astype(jnp.bfloat16).reshape(req_rows, width)
-        gathered = lax.all_gather(queries, "rep", axis=0, tiled=True)
+
+        def plan_vector(local, dev_axis):
+            heard = lax.axis_size(dev_axis)
+            piece_next = lax.axis_index(dev_axis)
+            m_next, y, row_out = (heard, piece_next, local.shape[0])
+            so_far_all = tuple(((h, (h + 1) % m_next) for h in range(m_next)))
+            grid = tuple(((h, (h - 1) % m_next) for h in range(m_next)))
+            all_values = jnp.zeros(
+                (*local.shape[:0], m_next * row_out, *local.shape[1:]), local.dtype
+            )
+            all_values = lax.dynamic_update_slice_in_dim(all_values, local, y * row_out, axis=0)
+            seen_now = upper = local
+            b_now = m_next // 2
+            for i0 in range(1, b_now + 1):
+                seen_now = lax.ppermute(seen_now, perm=so_far_all, axis_name=dev_axis)
+                all_values = lax.dynamic_update_slice_in_dim(
+                    all_values, seen_now, (y - i0) % m_next * row_out, axis=0
+                )
+                if i0 < m_next - b_now:
+                    upper = lax.ppermute(upper, dev_axis, grid)
+                    all_values = lax.dynamic_update_slice_in_dim(
+                        all_values, upper, (y + i0) % m_next * row_out, axis=0
+                    )
+            return all_values
+
+        gathered = plan_vector(queries, "rep")
         fresh = jnp.dot(
             pick_home,
             jnp.concatenate([new_keys, new_values], axis=1),

time: 1100 us -> 1110 us (level)
  blocking collectives: 741 us -> 716 us
  starting transfers between devices: 0.08 us -> 17.1 us
  waiting for transfers between devices: 0.05 us -> 12.6 us
    all_gather x2 -> x0, blocking collectives: 24.4 us -> none  [per_device(): gathered = lax.all_gather(queries, 'rep', axis=0, tiled=True)]
    ppermute x0 -> x6, starting transfers between devices: none -> 17.1 us  [the longest x2 8.78 us: plan_vector(): upper = lax.ppermute(upper, dev_axis, grid)]
    ppermute x0 -> x6, waiting for transfers between devices: none -> 12.5 us  [the longest x4 12.5 us: plan_vector(): seen_now = lax.ppermute(seen_now, perm=so_far_all, axis_name=dev_axis)]
  transfers between devices with their start and end apart: 2 -> 8, of which waited for: 0 -> 3; matrix products, arithmetic and copies ran while one was open for 0% -> 1% of each run, Pallas kernels for 0% -> 0%
where the time goes in v1:
time: 1110 us; the launch traced here: 1100 us
  blocking collectives  716 us (65%)
  local copies, waits for them, and re-layouts  275 us (25%)
  other arithmetic  44 us (4%)
  starting transfers between devices  17.1 us (2%)
  between operations  14.5 us (1%)
  waiting for transfers between devices  12.6 us (1%)
    all_gather x4, blocking collectives, combined_all(): pieces = jax.tree.map(lambda part: lax.all_gather(part, axis), value)  325 us
    dynamic_slice x254, local copies, waits for them, and re-layouts, combined_all(): lax.scan(lambda so_far, piece: (join(so_far, piece), None), head, tail)  215 us
    psum x2, blocking collectives, per_device(): qkv_full, inner = lax.psum((qkv_part, inner_part), 'blk')  180 us
    psum x2, blocking collectives, per_device(): average = lax.psum(jnp.sum(resid, axis=-1), 'blk') / D  101 us
    psum x2, blocking collectives, per_device(): variance = lax.psum(jnp.sum(centered * centered, axis=-1), 'blk') / D  91.6 us
    add x254, other arithmetic, merge_parts(): left_out * left_factor[..., None] + right_out * right_factor[..., None]  28.1 us
  transfers between devices with their start and end apart: 8, of which 3 were waited for; matrix products, arithmetic and copies ran while one was open for 1% of the time, Pallas kernels for 0%

profile of v1, /device:TPU:2, one launch (start us, length us, event | category | flops | bytes accessed | tf_op | source)
XLA Modules:
  0.0 1096.5 jit_solution(12080901201417976945)
XLA Ops:
  8.0 54.7 %psum.70 = f32[4]{0:T(128)S(1)} all-reduce(f32[4]{0:T(128)S(1)} %convert_reduce_fusion.1), channel_id=1, replica_groups=mesh['rep'=4,'blk'=32,'tp'=4] {'blk'}, use_global_device_ids=true, to_apply=%region_1.0 | all-reduce | flops 4 | bytes 32 | tf_op jit(solution)/shard_map/psum | solution.py:106
  62.8 0.9 fusion.97
  64.3 45.8 %psum.71 = f32[4]{0:T(128)S(1)} all-reduce(f32[4]{0:T(128)S(1)} %fusion.97), channel_id=1, replica_groups=mesh['rep'=4,'blk'=32,'tp'=4] {'blk'}, use_global_device_ids=true, to_apply=%region_3.0 | all-reduce | flops 4 | bytes 32 | tf_op jit(solution)/shard_map/psum | solution.py:108
  110.8 1.0 fusion.132
  112.1 1.2 fusion.20
  113.3 0.9 fusion.119
  114.3 90.1 %all-reduce.1 = (f32[4,3,8,64]{3,2,1,0:T(8,128)S(1)}, f32[4,2048]{1,0:T(4,128)}) all-reduce(f32[4,3,8,64]{3,2,1,0:T(8,128)S(1)} %reshape.328, f32[4,2048]{1,0:T(4,128)S(1)} %fusion.20), channel_id=1, replica_groups=mesh['rep'=4,'blk'=32,'tp'=4] {'blk'}, use_global_device_ids=true, to_apply=%region_4.0 | all-reduce | flops 14336 | bytes 114688 | tf_op jit(solution)/shard_map/psum | solution.py:118
  204.9 4.9 collective-permute-start.1
  209.8 1.9 collective-permute-start
  216.5 1.3 fusion.131
  218.9 2.5 collective-permute-start.2
  221.5 4.2 collective-permute-done.2
  227.2 0.9 fusion.47
  229.6 81.7 %all-gather.7 = f32[128,16,8]{1,2,0:T(8,128)S(1)} all-gather(f32[1,16,8]{1,2,0:T(8,128)S(1)} %convolution_bitcast_fusion.1), channel_id=3, replica_groups=mesh['rep'=4,'blk'=32,'tp'=4] {'rep','blk'}, dimensions={0}, use_global_device_ids=true | all-gather | bytes 66048 | tf_op jit(solution)/shard_map/all_gather | solution.py:16
  311.3 81.0 %all-gather.6 = f32[128,16,8]{1,2,0:T(8,128)S(1)} all-gather(f32[1,16,8]{1,2,0:T(8,128)S(1)} %bitcast.160), channel_id=2, replica_groups=mesh['rep'=4,'blk'=32,'tp'=4] {'rep','blk'}, dimensions={0}, use_global_device_ids=true | all-gather | bytes 66048 | tf_op jit(solution)/shard_map/all_gather | solution.py:16
  392.4 0.8 slice.231
  393.3 7.2 slice.234
  400.4 145.3 %while.28 = (s32[]{:T(128)}, f32[16,8]{0,1:T(8,128)S(1)}, f32[16,8]{0,1:T(8,128)S(1)}, f32[16,8,64]{2,1,0:T(8,128)S(1)}, f32[127,16,8]{1,2,0:T(8,128)S(1)}, /*in...) while((s32[]{:T(128)}, f32[16,8]{0,1:T(8,128)S(1)}, f32[16,8]{0,1:T(8,128)S(1)}, ...), condition=%wide.region_10.11_spmd, body=%wide.region_9.10_spmd.sunk | while | flops 25346 | bytes 171109 | solution.py:19
  400.6 0.9 constant_dynamic-slice_fusion.6
  406.4 0.8 constant_dynamic-slice_fusion.6
  412.1 0.8 constant_dynamic-slice_fusion.6
  417.8 0.8 constant_dynamic-slice_fusion.6
  428.1 0.8 constant_dynamic-slice_fusion.6
  433.8 0.8 constant_dynamic-slice_fusion.6
  439.5 0.8 constant_dynamic-slice_fusion.6
  449.8 0.8 constant_dynamic-slice_fusion.6
  455.6 0.8 constant_dynamic-slice_fusion.6
  461.3 0.8 constant_dynamic-slice_fusion.6
  471.6 0.8 constant_dynamic-slice_fusion.6
  477.3 0.8 constant_dynamic-slice_fusion.6
  483.0 0.8 constant_dynamic-slice_fusion.6
  493.3 0.8 constant_dynamic-slice_fusion.6
  499.0 0.8 constant_dynamic-slice_fusion.6
  504.7 0.8 constant_dynamic-slice_fusion.6
  515.0 0.8 constant_dynamic-slice_fusion.6
  520.7 0.8 constant_dynamic-slice_fusion.6
  526.5 0.8 constant_dynamic-slice_fusion.6
  536.8 0.8 constant_dynamic-slice_fusion.6
  542.5 0.8 constant_dynamic-slice_fusion.6
  546.2 1.1 convolution_add_fusion.1
  547.3 8.6 psum.74
  556.0 45.8 %psum.75 = f32[4]{0:T(128)S(1)} all-reduce(f32[4]{0:T(128)S(1)} %get-tuple-element.178), channel_id=1, replica_groups=mesh['rep'=4,'blk'=32,'tp'=4] {'blk'}, use_global_device_ids=true, to_apply=%region_14.15 | all-reduce | flops 4 | bytes 32 | tf_op jit(solution)/shard_map/psum | solution.py:106
  602.3 45.8 %psum.76 = f32[4]{0:T(128)S(1)} all-reduce(f32[4]{0:T(128)S(1)} %fusion.94), channel_id=1, replica_groups=mesh['rep'=4,'blk'=32,'tp'=4] {'blk'}, use_global_device_ids=true, to_apply=%region_16.17 | all-reduce | flops 4 | bytes 32 | tf_op jit(solution)/shard_map/psum | solution.py:108
  648.1 1.2 fusion.17
  649.3 1.1 fusion.122
  650.5 90.3 %all-reduce = (f32[4,3,8,64]{3,2,0,1:T(8,128)S(1)}, f32[4,2048]{1,0:T(4,128)S(1)}) all-reduce(f32[4,3,8,64]{3,2,0,1:T(8,128)S(1)} %copy.83, f32[4,2048]{1,0:T(4,128)S(1)} %fusion.17), channel_id=1, replica_groups=mesh['rep'=4,'blk'=32,'tp'=4] {'blk'}, use_global_device_ids=true, to_apply=%region_17.18 | all-reduce | flops 14336 | bytes 114688 | tf_op jit(solution)/shard_map/psum | solution.py:118
  741.2 3.9 collective-permute-start.4
  745.1 2.0 collective-permute-start.3
  748.2 3.6 collective-permute-done.3
  751.8 1.9 collective-permute-start.5
  753.8 4.7 collective-permute-done.5
  760.1 0.9 fusion.46
  761.3 1.1 pad_maximum_fusion
  762.6 79.6 %all-gather.9 = f32[128,16,8]{1,2,0:T(8,128)S(1)} all-gather(f32[1,16,8]{1,2,0:T(8,128)S(1)} %convolution_bitcast_fusion), channel_id=6, replica_groups=mesh['rep'=4,'blk'=32,'tp'=4] {'rep','blk'}, dimensions={0}, use_global_device_ids=true | all-gather | bytes 66048 | tf_op jit(solution)/shard_map/all_gather | solution.py:16
  842.3 82.9 %all-gather.8 = f32[128,16,8]{1,2,0:T(8,128)S(1)} all-gather(f32[1,16,8]{1,2,0:T(8,128)S(1)} %bitcast.159), channel_id=5, replica_groups=mesh['rep'=4,'blk'=32,'tp'=4] {'rep','blk'}, dimensions={0}, use_global_device_ids=true | all-gather | bytes 66048 | tf_op jit(solution)/shard_map/all_gather | solution.py:16
  925.3 0.8 slice.248
  926.2 7.2 slice.251
  933.4 144.9 %while.29 = (s32[]{:T(128)}, f32[16,8]{0,1:T(8,128)S(1)}, f32[16,8]{0,1:T(8,128)S(1)}, f32[16,8,64]{2,1,0:T(8,128)S(1)}, f32[127,16,8]{1,2,0:T(8,128)S(1)}, /*in...) while((s32[]{:T(128)}, f32[16,8]{0,1:T(8,128)S(1)}, f32[16,8]{0,1:T(8,128)S(1)}, ...), condition=%wide.region_23.24_spmd, body=%wide.region_22.23_spmd.sunk | while | flops 25346 | bytes 171109 | solution.py:19
  933.5 0.8 constant_dynamic-slice_fusion.7
  942.6 0.8 constant_dynamic-slice_fusion.7
  951.8 0.8 constant_dynamic-slice_fusion.7
  955.2 0.8 constant_dynamic-slice_fusion.7
  964.3 0.8 constant_dynamic-slice_fusion.7
  1078.9 10.2 psum.79
  (1384 shorter events, 279.7 us)
Async XLA Ops:
  7.2 218.5 %copy-start.4 = (s32[8]{0:T(128)S(1)}, s32[8]{0:T(128)}, u32[]{:S(2)}) copy-start(s32[8]{0:T(128)} %param.23) | copy-start | bytes 100
  7.2 385.2 %all-gather.13.cloned.1.call-start = ((), (), s32[]{:S(2)}) async-start(), calls=%async_computation | async-start | bytes 8454144 | tf_op jit(solution)/shard_map/all_gather | solution.py:16
  204.9 16.5 %collective-permute-start.1 = (bf16[4,512]{1,0:T(4,128)(2,1)S(1)}, bf16[4,512]{1,0:T(4,128)(2,1)S(1)}, u32[]{:S(2)}, u32[]{:S(2)}) collective-permute-start(bf16[4,512]{1,0:T(4,128)(2,1)S(1)} %convert_element_type.96), channel_id=1, source_target_pairs={{0,384},{128,0},{256,128},{384,256},{1,385},{129,1},{257,129},{385... | collective-permute-start | bytes 12296 | tf_op jit(solution)/shard_map/ppermute | solution.py:148
  209.8 9.1 collective-permute-start
  218.9 6.7 collective-permute-start.2
  228.2 697.1 %all-gather.15.cloned.1.call-start = ((), (), s32[]{:S(2)}) async-start(), calls=%async_computation.1 | async-start | bytes 8454144 | tf_op jit(solution)/shard_map/all_gather | solution.py:16
  393.2 152.8 %copy-start.1 = (bf16[2,512,64]{1,2,0:T(8,128)(2,1)S(1)}, bf16[2,512,64]{1,2,0:T(8,128)(2,1)}, u32[]{:S(2)}) copy-start(bf16[2,512,64]{1,2,0:T(8,128)(2,1)} %param.20) | copy-start | bytes 393220
  393.2 153.0 %copy-start.6 = (f32[4,2048]{1,0:T(4,128)S(1)}, f32[4,2048]{1,0:T(4,128)}, u32[]{:S(2)}) copy-start(f32[4,2048]{1,0:T(4,128)} %get-tuple-element.169) | copy-start | bytes 98308
  393.2 162.7 %copy-start.3 = (bf16[4,64]{1,0:T(4,128)(2,1)S(1)}, bf16[4,64]{1,0:T(4,128)(2,1)}, u32[]{:S(2)}) copy-start(bf16[4,64]{1,0:T(4,128)(2,1)} %param.16) | copy-start | bytes 1540
  400.4 360.6 %copy-start = (bf16[2,2,8,32,512]{4,3,2,1,0:T(8,128)(2,1)S(1)}, bf16[2,2,8,32,512]{4,3,2,1,0:T(8,128)(2,1)}, u32[]{:S(2)}) copy-start(bf16[2,2,8,32,512]{4,3,2,1,0:T(8,128)(2,1)} %param.22) | copy-start | bytes 3145732
  741.2 12.5 %collective-permute-start.4 = (bf16[4,512]{1,0:T(4,128)(2,1)S(1)}, bf16[4,512]{1,0:T(4,128)(2,1)S(1)}, u32[]{:S(2)}, u32[]{:S(2)}) collective-permute-start(bf16[4,512]{1,0:T(4,128)(2,1)S(1)} %convert_element_type.108), channel_id=1, source_target_pairs={{0,384},{128,0},{256,128},{384,256},{1,385},{129,1},{257,129},{385... | collective-permute-start | bytes 12296 | tf_op jit(solution)/shard_map/ppermute | solution.py:148
  745.1 6.7 collective-permute-start.3
  751.8 6.7 collective-permute-start.5
  926.2 152.4 %copy-start.2 = (bf16[2,512,64]{1,2,0:T(8,128)(2,1)S(1)}, bf16[2,512,64]{1,2,0:T(8,128)(2,1)}, u32[]{:S(2)}) copy-start(bf16[2,512,64]{1,2,0:T(8,128)(2,1)} %param.20) | copy-start | bytes 393220
  926.2 152.5 %copy-start.5 = (bf16[2,2048,64]{1,2,0:T(8,128)(2,1)S(1)}, bf16[2,2048,64]{1,2,0:T(8,128)(2,1)}, u32[]{:S(2)}) copy-start(bf16[2,2048,64]{1,2,0:T(8,128)(2,1)} %param.21) | copy-start | bytes 1572868
Sparse Core Ops, SparseCore 0:
  228.3 143.2 all-gather.12
  761.2 141.9 all-gather.14
